TPU v7x, 32 devices: a whole 2x2x4 slice. The times are simulated.
32 devices in a mesh: groups: 2 (over y), seq: 4 (over z), dp: 2 (over x), mp: 2 (over core).
Axes of the slice: x: 2, y: 2, z: 4, core: 2. Of those that a mesh axis runs over, the one named last changes fastest.
Arguments:
- queries: bfloat16 [4, 512, 2048], P(('groups', 'dp'), 'seq', 'mp'), parts along dimension 0, may hold values from -6 to 6
- keys: bfloat16 [4, 512, 2048], P(('groups', 'dp'), 'seq', 'mp'), parts along dimension 0, may hold values from -6 to 6
- values: bfloat16 [4, 512, 2048], P(('groups', 'dp'), 'seq', 'mp'), parts along dimension 0, may hold values from -6 to 6
- grad_output: bfloat16 [4, 512, 2048], P(('groups', 'dp'), 'seq', 'mp'), parts along dimension 0, may hold values from -6 to 6
- counts: int32 [4, 4, 4], P(('groups', 'dp'), 'seq'), parts along dimension 0, may hold values from 0 to 64, as said below
Outputs:
- grad_queries: bfloat16 [4, 512, 2048], P(('groups', 'dp'), 'seq', 'mp'), parts along dimension 0
- grad_keys: bfloat16 [4, 512, 2048], P(('groups', 'dp'), 'seq', 'mp'), parts along dimension 0
- grad_values: bfloat16 [4, 512, 2048], P(('groups', 'dp'), 'seq', 'mp'), parts along dimension 0
There are 2 independent parts, one for each index of `groups`. A program takes and returns all parts, laid end to end along the dimension named above; each array names one. Nothing has to cross between parts.
Inputs may be any that keep to these rules, and one draw needn't show every extreme that they name: Each shard's counts sum to 128; no entry exceeds 64, some window receives 64 points from every shard.
All inputs are finite; a program needn't handle non-finite values.
Results may differ from a plain program's by a relative error of at most 0.001.
Values may be sent and summed in bfloat16 or wider, within the bound.
A program may use at most 128 MiB of HBM per device.

v0:
```python
import math
import jax
import jax.numpy as jnp
from jax import lax
from jax.sharding import PartitionSpec as P

DH = 128
highest = lax.Precision.HIGHEST


def entering(value, axis, join, neutral, backward):
    count, mine = (lax.axis_size(axis), lax.axis_index(axis))
    pieces = lax.all_gather(value, axis)
    if backward:
        pieces = pieces[::-1]
        mine = count - 1 - mine
    total = jnp.full_like(value, 0) + jnp.asarray(neutral, value.dtype)

    def hop(position, total):
        longer = join(total, pieces[position])
        return jnp.where(position < mine, longer, total)

    return lax.fori_loop(0, count - 1, hop, total)


def add_states(earlier, later):
    return earlier + later


def per_device(queries, keys, values, grad_output, counts):
    shard_count = lax.axis_size("seq")
    local_rows = queries.shape[1]
    width = queries.shape[2]
    local_heads = width // DH
    capacity = 2 * local_rows // shard_count
    window_rows = shard_count * capacity
    factor = 1.0 / math.sqrt(DH * local_rows * shard_count)
    my_counts = counts[0, 0]
    window_ends = jnp.cumsum(my_counts)
    window_starts = window_ends - my_counts
    offsets = jnp.arange(capacity, dtype=jnp.int32)
    occupied = offsets[None, :] < my_counts[:, None]
    picked = jnp.where(occupied, window_starts[:, None] + offsets[None, :], 0).reshape(-1)
    occupied_column = occupied.reshape(-1, 1)

    def pack(source):
        taken = jnp.take(source[0], picked, axis=0)
        taken = jnp.where(occupied_column, taken, jnp.zeros_like(taken))
        return taken.reshape(shard_count, capacity, width)

    def split_heads(received):
        return received.reshape(window_rows, local_heads, DH)

    def outer_sum(left, right):
        return jnp.einsum("lha,lhb->hab", left, right, preferred_element_type=jnp.float32)

    query_recv, key_recv, value_recv, grad_recv = (
        lax.all_to_all(pack(queries), "seq", split_axis=0, concat_axis=0, tiled=True),
        lax.all_to_all(pack(keys), "seq", split_axis=0, concat_axis=0, tiled=True),
        lax.all_to_all(pack(values), "seq", split_axis=0, concat_axis=0, tiled=True),
        lax.all_to_all(pack(grad_output), "seq", split_axis=0, concat_axis=0, tiled=True),
    )
    query_recv = split_heads(query_recv)
    key_recv = split_heads(key_recv)
    value_recv = split_heads(value_recv)
    grad_recv = split_heads(grad_recv)
    key_state = outer_sum(key_recv, value_recv)
    query_state = outer_sum(query_recv, grad_recv)
    zero_state = jnp.zeros((local_heads, DH, DH), jnp.float32)
    before_kv = entering(key_state, "seq", add_states, zero_state, False)
    after_qd = entering(query_state, "seq", add_states, zero_state, True)
    block = min(512, window_rows)
    nblocks = window_rows // block

    def blocked(received):
        return received.reshape(nblocks, block, local_heads, DH)

    query_blocks = blocked(query_recv)
    key_blocks = blocked(key_recv)
    value_blocks = blocked(value_recv)
    grad_blocks = blocked(grad_recv)
    block_kv = jnp.einsum(
        "nlha,nlhb->nhab", key_blocks, value_blocks, preferred_element_type=jnp.float32
    )
    block_qd = jnp.einsum(
        "nlha,nlhb->nhab", query_blocks, grad_blocks, preferred_element_type=jnp.float32
    )
    kv_before = before_kv[None] + jnp.cumsum(block_kv, axis=0) - block_kv
    qd_after = after_qd[None] + jnp.sum(block_qd, axis=0)[None] - jnp.cumsum(block_qd, axis=0)
    lower = (
        lax.broadcasted_iota(jnp.int32, (block, block), 0)
        >= lax.broadcasted_iota(jnp.int32, (block, block), 1)
    ).astype(jnp.float32)

    def one_block(pieces):
        query_part, key_part, value_part, grad_part, kv_state, qd_state = pieces
        weights = (
            jnp.einsum("rha,sha->hrs", grad_part, value_part, preferred_element_type=jnp.float32)
            * lower[None]
        )
        scores = (
            jnp.einsum("rha,sha->hrs", query_part, key_part, preferred_element_type=jnp.float32)
            * lower[None]
        )
        query_f = query_part.astype(jnp.float32)
        key_f = key_part.astype(jnp.float32)
        value_f = value_part.astype(jnp.float32)
        grad_f = grad_part.astype(jnp.float32)
        grad_q = jnp.einsum("rhb,hab->rha", grad_f, kv_state, precision=highest) + jnp.einsum(
            "hrs,sha->rha", weights, key_f, precision=highest
        )
        grad_k = jnp.einsum("shb,hab->sha", value_f, qd_state, precision=highest) + jnp.einsum(
            "hrs,rha->sha", weights, query_f, precision=highest
        )
        grad_v = jnp.einsum("sha,hab->shb", key_f, qd_state, precision=highest) + jnp.einsum(
            "hrs,rhb->shb", scores, grad_f, precision=highest
        )

        def finish(result):
            return (result * factor).astype(jnp.bfloat16).reshape(block, width)

        return (finish(grad_q), finish(grad_k), finish(grad_v))

    out_q, out_k, out_v = lax.map(
        one_block, (query_blocks, key_blocks, value_blocks, grad_blocks, kv_before, qd_after)
    )

    def to_slots(result):
        return result.reshape(shard_count, capacity, width)

    back_q, back_k, back_v = (
        lax.all_to_all(to_slots(out_q), "seq", split_axis=0, concat_axis=0, tiled=True),
        lax.all_to_all(to_slots(out_k), "seq", split_axis=0, concat_axis=0, tiled=True),
        lax.all_to_all(to_slots(out_v), "seq", split_axis=0, concat_axis=0, tiled=True),
    )
    positions = jnp.arange(local_rows, dtype=jnp.int32)
    member = (
        (positions[:, None] >= window_starts[None, :]) & (positions[:, None] < window_ends[None, :])
    ).astype(jnp.int32)
    window_of = jnp.sum(member * jnp.arange(shard_count, dtype=jnp.int32)[None, :], axis=1)
    start_of = jnp.sum(member * window_starts[None, :], axis=1)
    source_index = window_of * capacity + positions - start_of

    def unpack(returned):
        return jnp.take(returned.reshape(window_rows, width), source_index, axis=0)[None]

    return (unpack(back_q), unpack(back_k), unpack(back_v))


def solution(mesh):
    placed = (
        P(("groups", "dp"), "seq", "mp"),
        P(("groups", "dp"), "seq", "mp"),
        P(("groups", "dp"), "seq", "mp"),
        P(("groups", "dp"), "seq", "mp"),
        P(("groups", "dp"), "seq", None),
    )
    return jax.shard_map(
        per_device,
        mesh=mesh,
        in_specs=placed,
        out_specs=(
            P(("groups", "dp"), "seq", "mp"),
            P(("groups", "dp"), "seq", "mp"),
            P(("groups", "dp"), "seq", "mp"),
        ),
        check_vma=False,
    )
```

profile of v0, /device:TPU:0, one launch (start us, length us, event | category | flops | bytes accessed | tf_op | source)
XLA Modules:
  0.0 218.9 jit_solution(3963657289021872831)
XLA Ops:
  14.5 1.3 select_select_fusion
  15.8 20.6 %all_to_all.35 = bf16[4,64,1024]{2,1,0:T(8,128)(2,1)S(1)} all-to-all(bf16[4,64,1024]{2,1,0:T(8,128)(2,1)S(1)} %bitcast.68), channel_id=1, replica_groups=mesh['groups'=2,'seq'=4,'dp'=2,'mp'=2] {'seq'}, dimensions={0} | all-to-all | bytes 1048576 | tf_op jit(solution)/shard_map/all_to_all | solution.py:61
  36.4 3.5 %all-to-all-start.4 = ((bf16[4,64,1024]{2,1,0:T(8,128)(2,1)}), bf16[4,64,1024]{2,1,0:T(8,128)(2,1)S(1)}, u32[]{:S(2)}, u32[]{:S(2)}) async-start(bf16[4,64,1024]{2,1,0:T(8,128)(2,1)} %bitcast.14), calls=%async_computation.4 | async-start | bytes 1048576 | tf_op jit(solution)/shard_map/all_to_all | solution.py:58
  40.4 13.1 %all-to-all-done.4 = bf16[4,64,1024]{2,1,0:T(8,128)(2,1)S(1)} async-done(((bf16[4,64,1024]{2,1,0:T(8,128)(2,1)}), bf16[4,64,1024]{2,1,0:T(8,128)(2,1)S(1)}, u32[]{:S(2)}, u32[]{:S(2)}) %all-to-all-start.4) | async-done | bytes 524320 | tf_op jit(solution)/shard_map/all_to_all | solution.py:58
  53.6 1.2 fusion.47
  54.8 27.9 %all_to_all.36 = bf16[4,64,1024]{2,1,0:T(8,128)(2,1)S(1)} all-to-all(bf16[4,64,1024]{2,1,0:T(8,128)(2,1)S(1)} %bitcast.67), channel_id=1, replica_groups=mesh['groups'=2,'seq'=4,'dp'=2,'mp'=2] {'seq'}, dimensions={0} | all-to-all | bytes 1048576 | tf_op jit(solution)/shard_map/all_to_all | solution.py:59
  82.7 4.1 %all-to-all-start.1 = ((bf16[4,64,1024]{2,1,0:T(8,128)(2,1)}), bf16[4,64,1024]{2,1,0:T(8,128)(2,1)S(1)}, u32[]{:S(2)}, u32[]{:S(2)}) async-start(bf16[4,64,1024]{2,1,0:T(8,128)(2,1)} %bitcast.6), calls=%async_computation.1 | async-start | bytes 1048576 | tf_op jit(solution)/shard_map/all_to_all | solution.py:60
  87.0 25.5 %all-to-all-done.1 = bf16[4,64,1024]{2,1,0:T(8,128)(2,1)S(1)} async-done(((bf16[4,64,1024]{2,1,0:T(8,128)(2,1)}), bf16[4,64,1024]{2,1,0:T(8,128)(2,1)S(1)}, u32[]{:S(2)}, u32[]{:S(2)}) %all-to-all-start.1) | async-done | bytes 524320 | tf_op jit(solution)/shard_map/all_to_all | solution.py:60
  113.3 2.2 fusion.55
  115.6 1.8 fusion.49
  117.4 3.2 %rev.3 = f32[4,8,128,128]{3,2,1,0:T(8,128)} reverse(f32[4,8,128,128]{3,2,1,0:T(8,128)} %bitcast.69), dimensions={0} | reverse | bytes 4194304 | tf_op jit(solution)/shard_map/rev | solution.py:15
  120.7 3.8 %while.35 = (s32[]{:T(128)}, f32[8,128,128]{2,1,0:T(8,128)S(1)}, s32[]{:T(128)}, f32[4,8,128,128]{3,2,1,0:T(8,128)}, s32[]{:T(128)}, /*index=5*/s32[]{:T(128)}) while((s32[]{:T(128)}, f32[8,128,128]{2,1,0:T(8,128)S(1)}, s32[]{:T(128)}, f32[4,8,128,128]{3,2,1,0:T(8,128)}, s32[]{:T(128)}, /*index=5*/s32[]{:T(128)}) %tuple.75), condition=%wide.region_6.9_spmd.clone, body=%wide.region_5.8_spmd.clone.sunk | while | flops 393220 | bytes 1572965 | solution.py:23
  120.7 1.3 add_select_fusion.5
  122.0 1.2 add_select_fusion.5
  123.2 1.3 add_select_fusion.5
  128.6 4.1 %all-to-all-start.6 = ((bf16[4,64,1024]{2,1,0:T(8,128)(2,1)}), bf16[4,64,1024]{2,1,0:T(8,128)(2,1)}, u32[]{:S(2)}, u32[]{:S(2)}) async-start(bf16[4,64,1024]{2,1,0:T(8,128)(2,1)} %reshape.172), calls=%async_computation.6 | async-start | bytes 1048576 | tf_op jit(solution)/shard_map/all_to_all | solution.py:134
  132.7 1.8 fusion.53
  134.5 1.7 fusion.51
  138.5 2.1 reshape.170
  140.6 21.8 %all-to-all-done.6 = bf16[4,64,1024]{2,1,0:T(8,128)(2,1)} async-done(((bf16[4,64,1024]{2,1,0:T(8,128)(2,1)}), bf16[4,64,1024]{2,1,0:T(8,128)(2,1)}, u32[]{:S(2)}, u32[]{:S(2)}) %all-to-all-start.6) | async-done | bytes 524320 | tf_op jit(solution)/shard_map/all_to_all | solution.py:134
  162.4 4.3 %all-to-all-start.5 = ((bf16[4,64,1024]{2,1,0:T(8,128)(2,1)}), bf16[4,64,1024]{2,1,0:T(8,128)(2,1)}, u32[]{:S(2)}, u32[]{:S(2)}) async-start(bf16[4,64,1024]{2,1,0:T(8,128)(2,1)} %reshape.170), calls=%async_computation.5 | async-start | bytes 1048576 | tf_op jit(solution)/shard_map/all_to_all | solution.py:133
  166.7 17.4 %all-gather.5.cloned.1.call-done = f32[32,128,128]{2,1,0:T(8,128)} async-done(((f32[8,128,128]{2,1,0:T(8,128)}), f32[32,128,128]{2,1,0:T(8,128)}) %all-gather.5.cloned.1.call-update) | async-done | bytes 2097168 | tf_op jit(solution)/shard_map/all_gather | solution.py:13
  184.1 3.8 %while.34 = (s32[]{:T(128)}, f32[8,128,128]{2,1,0:T(8,128)S(1)}, s32[]{:T(128)}, f32[4,8,128,128]{3,2,1,0:T(8,128)}, s32[]{:T(128)}, /*index=5*/s32[]{:T(128)}) while((s32[]{:T(128)}, f32[8,128,128]{2,1,0:T(8,128)S(1)}, s32[]{:T(128)}, f32[4,8,128,128]{3,2,1,0:T(8,128)}, s32[]{:T(128)}, /*index=5*/s32[]{:T(128)}) %tuple.85), condition=%wide.region_2.4_spmd.clone, body=%wide.region_1.3_spmd.clone.sunk | while | flops 393220 | bytes 1572965 | solution.py:23
  184.1 1.3 add_select_fusion.4
  185.4 1.2 add_select_fusion.4
  186.7 1.2 add_select_fusion.4
  187.9 1.7 fusion.45
  189.6 1.4 fusion.33
  192.5 3.5 %all-to-all-start.3 = ((bf16[4,64,1024]{2,1,0:T(8,128)(2,1)}), bf16[4,64,1024]{2,1,0:T(8,128)(2,1)S(1)}, u32[]{:S(2)}, u32[]{:S(2)}) async-start(bf16[4,64,1024]{2,1,0:T(8,128)(2,1)} %reshape.166), calls=%async_computation.3 | async-start | bytes 1048576 | tf_op jit(solution)/shard_map/all_to_all | solution.py:132
  196.0 2.2 gather_fusion.6
  198.2 2.2 gather_fusion.5
  200.4 9.9 %all-to-all-done.3 = bf16[4,64,1024]{2,1,0:T(8,128)(2,1)S(1)} async-done(((bf16[4,64,1024]{2,1,0:T(8,128)(2,1)}), bf16[4,64,1024]{2,1,0:T(8,128)(2,1)S(1)}, u32[]{:S(2)}, u32[]{:S(2)}) %all-to-all-start.3) | async-done | bytes 524320 | tf_op jit(solution)/shard_map/all_to_all | solution.py:132
  (71 shorter events, 18.5 us)
Async XLA Ops:
  7.2 2.5 %copy-start = (bf16[1,128,1024]{2,1,0:T(8,128)(2,1)S(1)}, bf16[1,128,1024]{2,1,0:T(8,128)(2,1)}, u32[]{:S(2)}) copy-start(bf16[1,128,1024]{2,1,0:T(8,128)(2,1)} %param.13) | copy-start | bytes 786436
  9.7 1.2 copy-start.1
  10.9 1.2 copy-start.2
  12.1 1.2 copy-start.3
  36.4 17.1 %all-to-all-start.4 = ((bf16[4,64,1024]{2,1,0:T(8,128)(2,1)}), bf16[4,64,1024]{2,1,0:T(8,128)(2,1)S(1)}, u32[]{:S(2)}, u32[]{:S(2)}) async-start(bf16[4,64,1024]{2,1,0:T(8,128)(2,1)} %bitcast.14), calls=%async_computation.4 | async-start | bytes 1048576 | tf_op jit(solution)/shard_map/all_to_all | solution.py:58
  39.9 77.6 %all-gather.7.cloned.1.call-start = ((), (), s32[]{:S(2)}) async-start(), calls=%async_computation.8 | async-start | bytes 2621440 | tf_op jit(solution)/shard_map/all_gather | solution.py:13
  40.3 84.8 %copy-start.4 = (bf16[256,8,128]{0,2,1:T(8,128)(2,1)}, bf16[256,8,128]{0,2,1:T(8,128)(2,1)S(1)}, u32[]{:S(2)}) copy-start(bf16[256,8,128]{0,2,1:T(8,128)(2,1)S(1)} %copy.66) | copy-start | bytes 1572868
  53.6 62.0 %copy-start.10 = (bf16[32,8,8,128]{3,2,1,0:T(8,128)(2,1)}, bf16[32,8,8,128]{3,2,1,0:T(8,128)(2,1)S(1)}, u32[]{:S(2)}) copy-start(bf16[32,8,8,128]{3,2,1,0:T(8,128)(2,1)S(1)} %copy.72) | copy-start | bytes 1572868
  82.7 29.7 %all-to-all-start.1 = ((bf16[4,64,1024]{2,1,0:T(8,128)(2,1)}), bf16[4,64,1024]{2,1,0:T(8,128)(2,1)S(1)}, u32[]{:S(2)}, u32[]{:S(2)}) async-start(bf16[4,64,1024]{2,1,0:T(8,128)(2,1)} %bitcast.6), calls=%async_computation.1 | async-start | bytes 1048576 | tf_op jit(solution)/shard_map/all_to_all | solution.py:60
  86.9 97.3 %all-gather.5.cloned.1.call-start = ((), (), s32[]{:S(2)}) async-start(), calls=%async_computation.7 | async-start | bytes 2621440 | tf_op jit(solution)/shard_map/all_gather | solution.py:13
  87.0 37.5 %copy-start.6 = (bf16[32,8,8,128]{3,2,1,0:T(8,128)(2,1)}, bf16[32,8,8,128]{3,2,1,0:T(8,128)(2,1)S(1)}, u32[]{:S(2)}) copy-start(bf16[32,8,8,128]{3,2,1,0:T(8,128)(2,1)S(1)} %copy.69) | copy-start | bytes 1572868
  115.6 9.5 %copy-start.13 = (f32[256,256]{1,0:T(8,128)}, f32[256,256]{1,0:T(8,128)S(1)}, u32[]{:S(2)}) copy-start(f32[256,256]{1,0:T(8,128)S(1)} %fusion.62) | copy-start | bytes 786436
  120.7 3.9 %copy-start.8 = (f32[8,128,128]{2,1,0:T(8,128)S(1)}, f32[8,128,128]{2,1,0:T(8,128)}, u32[]{:S(2)}) copy-start(f32[8,128,128]{2,1,0:T(8,128)} %fusion.47) | copy-start | bytes 1572868
  124.5 1.7 copy-start.12
  128.6 33.8 %all-to-all-start.6 = ((bf16[4,64,1024]{2,1,0:T(8,128)(2,1)}), bf16[4,64,1024]{2,1,0:T(8,128)(2,1)}, u32[]{:S(2)}, u32[]{:S(2)}) async-start(bf16[4,64,1024]{2,1,0:T(8,128)(2,1)} %reshape.172), calls=%async_computation.6 | async-start | bytes 1048576 | tf_op jit(solution)/shard_map/all_to_all | solution.py:134
  132.7 1.8 copy-start.9
  134.5 1.7 copy-start.11
  134.5 1.7 copy-start.14
  162.4 30.1 %all-to-all-start.5 = ((bf16[4,64,1024]{2,1,0:T(8,128)(2,1)}), bf16[4,64,1024]{2,1,0:T(8,128)(2,1)}, u32[]{:S(2)}, u32[]{:S(2)}) async-start(bf16[4,64,1024]{2,1,0:T(8,128)(2,1)} %reshape.170), calls=%async_computation.5 | async-start | bytes 1048576 | tf_op jit(solution)/shard_map/all_to_all | solution.py:133
  184.1 3.8 %copy-start.5 = (bf16[256,8,128]{0,2,1:T(8,128)(2,1)S(1)}, bf16[256,8,128]{0,2,1:T(8,128)(2,1)}, u32[]{:S(2)}) copy-start(bf16[256,8,128]{0,2,1:T(8,128)(2,1)} %copy-done.4) | copy-start | bytes 1572868
  187.9 1.7 copy-start.7
  187.9 1.7 copy-start.15
  192.5 17.8 %all-to-all-start.3 = ((bf16[4,64,1024]{2,1,0:T(8,128)(2,1)}), bf16[4,64,1024]{2,1,0:T(8,128)(2,1)S(1)}, u32[]{:S(2)}, u32[]{:S(2)}) async-start(bf16[4,64,1024]{2,1,0:T(8,128)(2,1)} %reshape.166), calls=%async_computation.3 | async-start | bytes 1048576 | tf_op jit(solution)/shard_map/all_to_all | solution.py:132
Sparse Core Ops, SparseCore 0:
  54.9 61.5 all-gather.6
  118.1 65.9 all-gather.4
where the time goes:
time: 220 us; the launch traced here: 219 us
  waiting for transfers between devices  87.7 us (40%)
  blocking collectives  48.5 us (22%)
  local copies, waits for them, and re-layouts  21.6 us (10%)
  starting transfers between devices  19.6 us (9%)
  matrix products  14.6 us (7%)
  between operations  14.5 us (7%)
  other arithmetic  12.3 us (6%)
    all_to_all x1, blocking collectives, per_device(): lax.all_to_all(pack(keys), 'seq', split_axis=0, concat_axis=0, tiled=True)  27.9 us
    all_to_all x1, waiting for transfers between devices, per_device(): lax.all_to_all(pack(values), 'seq', split_axis=0, concat_axis=0, tiled=True)  25.5 us
    all_to_all x1, waiting for transfers between devices, per_device(): lax.all_to_all(to_slots(out_v), 'seq', split_axis=0, concat_axis=0, tiled...  21.8 us
    all_to_all x1, blocking collectives, per_device(): lax.all_to_all(pack(grad_output), 'seq', split_axis=0, concat_axis=0, til...  20.6 us
    all_gather x2, waiting for transfers between devices, entering(): pieces = lax.all_gather(value, axis)  17.4 us
    all_to_all x1, waiting for transfers between devices, per_device(): lax.all_to_all(pack(queries), 'seq', split_axis=0, concat_axis=0, tiled=T...  13.1 us
    all_to_all x1, waiting for transfers between devices, per_device(): lax.all_to_all(to_slots(out_q), 'seq', split_axis=0, concat_axis=0, tiled...  9.87 us
    select_n x6, other arithmetic, hop(): return jnp.where(position < mine, longer, total)  7.5 us
  transfers between devices with their start and end apart: 7, of which 5 were waited for; matrix products, arithmetic and copies ran while one was open for 16% of the time, Pallas kernels for 0%

commit v1 on v0

--- a/solution.py
+++ b/solution.py
@@ -6,6 +6,30 @@
 
 DH = 128
 highest = lax.Precision.HIGHEST
+
+
+def in_blocks(value, dim, peers):
+    shape = value.shape
+    blocks = value.reshape(*shape[:dim], peers, shape[dim] // peers, *shape[dim + 1 :])
+    return jnp.moveaxis(blocks, dim, 0)
+
+
+def joined_along(blocks, dim):
+    blocks = jnp.moveaxis(blocks, 0, dim)
+    dims = blocks.shape
+    return blocks.reshape(*dims[:dim], dims[dim] * dims[dim + 1], *dims[dim + 2 :])
+
+
+def sent_to_each(array, axis, split_dim, concat_dim):
+    count, index = (lax.axis_size(axis), lax.axis_index(axis))
+    tiles = in_blocks(array, split_dim, count)
+    out = tiles
+    for turn in range(1, count):
+        target, source = ((index + turn) % count, (index - turn) % count)
+        sent = lax.dynamic_index_in_dim(tiles, target, 0)
+        received = lax.ppermute(sent, axis, [(i, (i + turn) % count) for i in range(count)])
+        out = lax.dynamic_update_slice_in_dim(out, received, source, axis=0)
+    return joined_along(out, concat_dim)
 
 
 def entering(value, axis, join, neutral, backward):
@@ -131,7 +155,7 @@
     back_q, back_k, back_v = (
         lax.all_to_all(to_slots(out_q), "seq", split_axis=0, concat_axis=0, tiled=True),
         lax.all_to_all(to_slots(out_k), "seq", split_axis=0, concat_axis=0, tiled=True),
-        lax.all_to_all(to_slots(out_v), "seq", split_axis=0, concat_axis=0, tiled=True),
+        sent_to_each(to_slots(out_v), "seq", 0, 0),
     )
     positions = jnp.arange(local_rows, dtype=jnp.int32)
     member = (

time: 220 us -> 223 us (1.014)
  waiting for transfers between devices: 87.7 us -> 84.5 us
  local copies, waits for them, and re-layouts: 21.6 us -> 24.2 us
    all_to_all x1 -> x0, waiting for transfers between devices: 21.8 us -> none  [per_device(): lax.all_to_all(to_slots(out_v), 'seq', split_axis=0, concat_axis=0, tiled...]
    ppermute x0 -> x3, waiting for transfers between devices: none -> 15.9 us  [sent_to_each(): lax.ppermute(sent, axis, [(i, (i + turn) % count) for i in range(count)])]
    all_gather x2, waiting for transfers between devices: 17.4 us -> 30 us  [entering(): pieces = lax.all_gather(value, axis)]
    all_to_all x1, waiting for transfers between devices: 9.87 us -> 0.01 us  [per_device(): lax.all_to_all(to_slots(out_q), 'seq', split_axis=0, concat_axis=0, tiled...]
    ppermute x0 -> x3, starting transfers between devices: none -> 4.51 us  [sent_to_each(): lax.ppermute(sent, axis, [(i, (i + turn) % count) for i in range(count)])]
    all_to_all x1 -> x0, starting transfers between devices: 4.14 us -> none  [per_device(): lax.all_to_all(to_slots(out_v), 'seq', split_axis=0, concat_axis=0, tiled...]
  transfers between devices with their start and end apart: 7 -> 9, of which waited for: 5 -> 4; matrix products, arithmetic and copies ran while one was open for 16% -> 19% of each run, Pallas kernels for 0% -> 0%
where the time goes in v1:
time: 223 us; the launch traced here: 222 us
  waiting for transfers between devices  84.5 us (38%)
  blocking collectives  48.5 us (22%)
  local copies, waits for them, and re-layouts  24.2 us (11%)
  starting transfers between devices  20.7 us (9%)
  matrix products  16.5 us (7%)
  between operations  14.5 us (7%)
  other arithmetic  13 us (6%)
    all_gather x2, waiting for transfers between devices, entering(): pieces = lax.all_gather(value, axis)  30 us
    all_to_all x1, blocking collectives, per_device(): lax.all_to_all(pack(keys), 'seq', split_axis=0, concat_axis=0, tiled=True)  27.9 us
    all_to_all x1, waiting for transfers between devices, per_device(): lax.all_to_all(pack(values), 'seq', split_axis=0, concat_axis=0, tiled=True)  25.5 us
    all_to_all x1, blocking collectives, per_device(): lax.all_to_all(pack(grad_output), 'seq', split_axis=0, concat_axis=0, til...  20.6 us
    ppermute x3, waiting for transfers between devices, sent_to_each(): lax.ppermute(sent, axis, [(i, (i + turn) % count) for i in range(count)])  15.9 us
    all_to_all x1, waiting for transfers between devices, per_device(): lax.all_to_all(pack(queries), 'seq', split_axis=0, concat_axis=0, tiled=T...  13.1 us
    select_n x6, other arithmetic, hop(): return jnp.where(position < mine, longer, total)  7.47 us
    all_to_all x1, starting transfers between devices, per_device(): lax.all_to_all(to_slots(out_k), 'seq', split_axis=0, concat_axis=0, tiled...  5.07 us
  transfers between devices with their start and end apart: 9, of which 4 were waited for; matrix products, arithmetic and copies ran while one was open for 19% of the time, Pallas kernels for 0%

profile of v1, /device:TPU:0, one launch (start us, length us, event | category | flops | bytes accessed | tf_op | source)
XLA Modules:
  0.0 222.0 jit_solution(5695558334169814718)
XLA Ops:
  14.5 1.3 select_select_fusion
  15.8 20.6 %all_to_all.30 = bf16[4,64,1024]{2,1,0:T(8,128)(2,1)S(1)} all-to-all(bf16[4,64,1024]{2,1,0:T(8,128)(2,1)S(1)} %bitcast.72), channel_id=1, replica_groups=mesh['groups'=2,'seq'=4,'dp'=2,'mp'=2] {'seq'}, dimensions={0} | all-to-all | bytes 1048576 | tf_op jit(solution)/shard_map/all_to_all | solution.py:85
  36.4 3.5 %all-to-all-start.4 = ((bf16[4,64,1024]{2,1,0:T(8,128)(2,1)}), bf16[4,64,1024]{2,1,0:T(8,128)(2,1)S(1)}, u32[]{:S(2)}, u32[]{:S(2)}) async-start(bf16[4,64,1024]{2,1,0:T(8,128)(2,1)} %bitcast.14), calls=%async_computation.4 | async-start | bytes 1048576 | tf_op jit(solution)/shard_map/all_to_all | solution.py:82
  40.3 13.1 %all-to-all-done.4 = bf16[4,64,1024]{2,1,0:T(8,128)(2,1)S(1)} async-done(((bf16[4,64,1024]{2,1,0:T(8,128)(2,1)}), bf16[4,64,1024]{2,1,0:T(8,128)(2,1)S(1)}, u32[]{:S(2)}, u32[]{:S(2)}) %all-to-all-start.4) | async-done | bytes 524320 | tf_op jit(solution)/shard_map/all_to_all | solution.py:82
  54.7 27.9 %all_to_all.31 = bf16[4,64,1024]{2,1,0:T(8,128)(2,1)S(1)} all-to-all(bf16[4,64,1024]{2,1,0:T(8,128)(2,1)S(1)} %bitcast.71), channel_id=1, replica_groups=mesh['groups'=2,'seq'=4,'dp'=2,'mp'=2] {'seq'}, dimensions={0} | all-to-all | bytes 1048576 | tf_op jit(solution)/shard_map/all_to_all | solution.py:83
  82.7 4.1 %all-to-all-start.1 = ((bf16[4,64,1024]{2,1,0:T(8,128)(2,1)}), bf16[4,64,1024]{2,1,0:T(8,128)(2,1)S(1)}, u32[]{:S(2)}, u32[]{:S(2)}) async-start(bf16[4,64,1024]{2,1,0:T(8,128)(2,1)} %bitcast.6), calls=%async_computation.1 | async-start | bytes 1048576 | tf_op jit(solution)/shard_map/all_to_all | solution.py:84
  86.9 25.5 %all-to-all-done.1 = bf16[4,64,1024]{2,1,0:T(8,128)(2,1)S(1)} async-done(((bf16[4,64,1024]{2,1,0:T(8,128)(2,1)}), bf16[4,64,1024]{2,1,0:T(8,128)(2,1)S(1)}, u32[]{:S(2)}, u32[]{:S(2)}) %all-to-all-start.1) | async-done | bytes 524320 | tf_op jit(solution)/shard_map/all_to_all | solution.py:84
  115.3 1.8 fusion.49
  117.1 1.5 fusion.53
  118.7 3.2 %rev.3 = f32[4,8,128,128]{3,2,1,0:T(8,128)} reverse(f32[4,8,128,128]{3,2,1,0:T(8,128)} %bitcast.73), dimensions={0} | reverse | bytes 4194304 | tf_op jit(solution)/shard_map/rev | solution.py:39
  121.9 3.8 %while.35 = (s32[]{:T(128)}, f32[8,128,128]{2,1,0:T(8,128)S(1)}, s32[]{:T(128)}, f32[4,8,128,128]{3,2,1,0:T(8,128)}, s32[]{:T(128)}, /*index=5*/s32[]{:T(128)}) while((s32[]{:T(128)}, f32[8,128,128]{2,1,0:T(8,128)S(1)}, s32[]{:T(128)}, f32[4,8,128,128]{3,2,1,0:T(8,128)}, s32[]{:T(128)}, /*index=5*/s32[]{:T(128)}) %tuple.77), condition=%wide.region_6.9_spmd.clone, body=%wide.region_5.8_spmd.clone.sunk | while | flops 393220 | bytes 1572965 | solution.py:47
  123.1 1.3 add_select_fusion.5
  124.4 1.3 add_select_fusion.5
  125.7 2.0 fusion.60
  127.8 2.8 %fusion.39 = bf16[256,8,128]{0,2,1:T(8,128)(2,1)} fusion(f32[8,128,256]{2,1,0:T(8,128)S(1)} %fusion.60, bf16[256,8,128]{0,2,1:T(8,128)(2,1)S(1)} %copy-done.6, f32[8,256,256]{2,1,0:T(8,128)S(1)} %copy-done.14, f32[256,256]{1,0:T(8,128)} %fusion.62), kind=kOutput, calls=%fused_computation.26 | convolution fusion | flops 806617088 | bytes 4456448 | tf_op jit(solution)/shard_map/while/body/eval_jaxpr/hrs,rhb->shb/dot_general | solution.py:139
  130.6 2.1 copy.67
  132.7 2.1 reshape_reshape.4
  135.8 1.8 fusion.51
  139.9 2.1 reshape.164
  142.0 5.1 %all-to-all-start.5 = ((bf16[4,64,1024]{2,1,0:T(8,128)(2,1)}), bf16[4,64,1024]{2,1,0:T(8,128)(2,1)}, u32[]{:S(2)}, u32[]{:S(2)}) async-start(bf16[4,64,1024]{2,1,0:T(8,128)(2,1)} %reshape.164), calls=%async_computation.5 | async-start | bytes 1048576 | tf_op jit(solution)/shard_map/all_to_all | solution.py:157
  147.0 30.0 %all-gather.5.cloned.1.call-done = f32[32,128,128]{2,1,0:T(8,128)} async-done(((f32[8,128,128]{2,1,0:T(8,128)}), f32[32,128,128]{2,1,0:T(8,128)}) %all-gather.5.cloned.1.call-update) | async-done | bytes 2097168 | tf_op jit(solution)/shard_map/all_gather | solution.py:37
  177.0 3.8 %while.34 = (s32[]{:T(128)}, f32[8,128,128]{2,1,0:T(8,128)S(1)}, s32[]{:T(128)}, f32[4,8,128,128]{3,2,1,0:T(8,128)}, s32[]{:T(128)}, /*index=5*/s32[]{:T(128)}) while((s32[]{:T(128)}, f32[8,128,128]{2,1,0:T(8,128)S(1)}, s32[]{:T(128)}, f32[4,8,128,128]{3,2,1,0:T(8,128)}, s32[]{:T(128)}, /*index=5*/s32[]{:T(128)}) %tuple.87), condition=%wide.region_2.4_spmd.clone, body=%wide.region_1.3_spmd.clone.sunk | while | flops 393220 | bytes 1572965 | solution.py:47
  177.0 1.3 add_select_fusion.4
  178.3 1.2 add_select_fusion.4
  179.6 1.2 add_select_fusion.4
  180.8 1.7 fusion.45
  182.5 1.4 fusion.33
  185.3 3.5 %all-to-all-start.3 = ((bf16[4,64,1024]{2,1,0:T(8,128)(2,1)}), bf16[4,64,1024]{2,1,0:T(8,128)(2,1)S(1)}, u32[]{:S(2)}, u32[]{:S(2)}) async-start(bf16[4,64,1024]{2,1,0:T(8,128)(2,1)} %reshape.160), calls=%async_computation.3 | async-start | bytes 1048576 | tf_op jit(solution)/shard_map/all_to_all | solution.py:156
  189.9 3.0 %collective-permute-start.1 = (bf16[1,1,64,1024]{3,2,0,1:T(8,128)(2,1)S(1)}, bf16[1,1,64,1024]{3,2,0,1:T(8,128)(2,1)S(1)}, u32[]{:S(2)}, u32[]{:S(2)}) collective-permute-start(bf16[1,1,64,1024]{3,2,0,1:T(8,128)(2,1)S(1)} %get-tuple-element.251), channel_id=1, source_target_pairs={{0,8},{4,12},{8,0},{12,4},{1,9},{5,13},{9,1},{13,5},{2,10},{6,14},... | collective-permute-start | bytes 393224 | tf_op jit(solution)/shard_map/ppermute | solution.py:30
  192.8 1.5 collective-permute-start.2
  194.3 15.8 %collective-permute-done.1 = bf16[1,1,64,1024]{3,2,0,1:T(8,128)(2,1)S(1)} collective-permute-done((bf16[1,1,64,1024]{3,2,0,1:T(8,128)(2,1)S(1)}, bf16[1,1,64,1024]{3,2,0,1:T(8,128)(2,1)S(1)}, u32[]{:S(2)}, u32[]{:S(2)}) %collective-permute-start.1) | collective-permute-done | bytes 131104 | tf_op jit(solution)/shard_map/ppermute | solution.py:30
  211.1 2.2 gather_fusion.5
  (81 shorter events, 21.6 us)
Async XLA Ops:
  7.2 2.5 %copy-start = (bf16[1,128,1024]{2,1,0:T(8,128)(2,1)S(1)}, bf16[1,128,1024]{2,1,0:T(8,128)(2,1)}, u32[]{:S(2)}) copy-start(bf16[1,128,1024]{2,1,0:T(8,128)(2,1)} %param.13) | copy-start | bytes 786436
  9.7 1.2 copy-start.1
  10.9 1.2 copy-start.2
  12.1 1.2 copy-start.3
  36.4 17.1 %all-to-all-start.4 = ((bf16[4,64,1024]{2,1,0:T(8,128)(2,1)}), bf16[4,64,1024]{2,1,0:T(8,128)(2,1)S(1)}, u32[]{:S(2)}, u32[]{:S(2)}) async-start(bf16[4,64,1024]{2,1,0:T(8,128)(2,1)} %bitcast.14), calls=%async_computation.4 | async-start | bytes 1048576 | tf_op jit(solution)/shard_map/all_to_all | solution.py:82
  39.8 78.8 %all-gather.7.cloned.1.call-start = ((), (), s32[]{:S(2)}) async-start(), calls=%async_computation.7 | async-start | bytes 2621440 | tf_op jit(solution)/shard_map/all_gather | solution.py:37
  40.3 42.3 %copy-start.5 = (bf16[256,8,128]{0,2,1:T(8,128)(2,1)}, bf16[256,8,128]{0,2,1:T(8,128)(2,1)S(1)}, u32[]{:S(2)}) copy-start(bf16[256,8,128]{0,2,1:T(8,128)(2,1)S(1)} %copy.66) | copy-start | bytes 1572868
  53.5 61.7 %copy-start.10 = (bf16[32,8,8,128]{3,2,1,0:T(8,128)(2,1)}, bf16[32,8,8,128]{3,2,1,0:T(8,128)(2,1)S(1)}, u32[]{:S(2)}) copy-start(bf16[32,8,8,128]{3,2,1,0:T(8,128)(2,1)S(1)} %copy.72) | copy-start | bytes 1572868
  82.7 29.7 %all-to-all-start.1 = ((bf16[4,64,1024]{2,1,0:T(8,128)(2,1)}), bf16[4,64,1024]{2,1,0:T(8,128)(2,1)S(1)}, u32[]{:S(2)}, u32[]{:S(2)}) async-start(bf16[4,64,1024]{2,1,0:T(8,128)(2,1)} %bitcast.6), calls=%async_computation.1 | async-start | bytes 1048576 | tf_op jit(solution)/shard_map/all_to_all | solution.py:84
  86.8 90.2 %all-gather.5.cloned.1.call-start = ((), (), s32[]{:S(2)}) async-start(), calls=%async_computation.6 | async-start | bytes 2621440 | tf_op jit(solution)/shard_map/all_gather | solution.py:37
  86.9 28.4 %copy-start.8 = (bf16[32,8,8,128]{3,2,1,0:T(8,128)(2,1)}, bf16[32,8,8,128]{3,2,1,0:T(8,128)(2,1)S(1)}, u32[]{:S(2)}) copy-start(bf16[32,8,8,128]{3,2,1,0:T(8,128)(2,1)S(1)} %copy.69) | copy-start | bytes 1572868
  112.5 0.8 copy-start.12
  114.5 2.6 %copy-start.13 = (bf16[32,8,8,128]{3,2,1,0:T(8,128)(2,1)S(1)}, bf16[32,8,8,128]{3,2,1,0:T(8,128)(2,1)}, u32[]{:S(2)}) copy-start(bf16[32,8,8,128]{3,2,1,0:T(8,128)(2,1)} %copy-done.12) | copy-start | bytes 1572868
  125.7 2.0 copy-start.6
  125.7 2.1 copy-start.14
  134.8 2.9 %copy-start.11 = (bf16[32,8,8,128]{3,2,1,0:T(8,128)(2,1)S(1)}, bf16[32,8,8,128]{3,2,1,0:T(8,128)(2,1)}, u32[]{:S(2)}) copy-start(bf16[32,8,8,128]{3,2,1,0:T(8,128)(2,1)} %copy-done.10) | copy-start | bytes 1572868
  134.8 2.9 %copy-start.15 = (f32[256,256]{1,0:T(8,128)S(1)}, f32[256,256]{1,0:T(8,128)}, u32[]{:S(2)}) copy-start(f32[256,256]{1,0:T(8,128)} %fusion.62) | copy-start | bytes 786436
  135.8 53.2 %collective-permute-start = (bf16[1,1,64,1024]{3,2,0,1:T(8,128)(2,1)S(1)}, bf16[1,1,64,1024]{3,2,0,1:T(8,128)(2,1)}, u32[]{:S(2)}, u32[]{:S(2)}) collective-permute-start(bf16[1,1,64,1024]{3,2,0,1:T(8,128)(2,1)S(1)} %constant_dynamic-slice_fusion.2), channel_id=1, source_target_pairs={{0,4},{4,8},{8,12},{12,0},{1,5},{5,9},{9,13},{13,1},{2,6},{6,10},{... | collective-permute-start | bytes 393224 | tf_op jit(solution)/shard_map/ppermute | solution.py:30
  142.0 43.4 %all-to-all-start.5 = ((bf16[4,64,1024]{2,1,0:T(8,128)(2,1)}), bf16[4,64,1024]{2,1,0:T(8,128)(2,1)}, u32[]{:S(2)}, u32[]{:S(2)}) async-start(bf16[4,64,1024]{2,1,0:T(8,128)(2,1)} %reshape.164), calls=%async_computation.5 | async-start | bytes 1048576 | tf_op jit(solution)/shard_map/all_to_all | solution.py:157
  177.0 3.8 %copy-start.7 = (bf16[256,8,128]{0,2,1:T(8,128)(2,1)S(1)}, bf16[256,8,128]{0,2,1:T(8,128)(2,1)}, u32[]{:S(2)}) copy-start(bf16[256,8,128]{0,2,1:T(8,128)(2,1)} %copy-done.5) | copy-start | bytes 1572868
  180.8 1.7 copy-start.9
  180.8 1.7 copy-start.16
  184.0 4.9 %copy-start.4 = (bf16[4,1,64,1024]{3,2,0,1:T(8,128)(2,1)S(1)}, bf16[4,1,64,1024]{3,2,0,1:T(8,128)(2,1)}, u32[]{:S(2)}) copy-start(bf16[4,1,64,1024]{3,2,0,1:T(8,128)(2,1)} %reshape_reshape.4) | copy-start | bytes 1572868
  185.3 27.9 %all-to-all-start.3 = ((bf16[4,64,1024]{2,1,0:T(8,128)(2,1)}), bf16[4,64,1024]{2,1,0:T(8,128)(2,1)S(1)}, u32[]{:S(2)}, u32[]{:S(2)}) async-start(bf16[4,64,1024]{2,1,0:T(8,128)(2,1)} %reshape.160), calls=%async_computation.3 | async-start | bytes 1048576 | tf_op jit(solution)/shard_map/all_to_all | solution.py:156
  189.9 20.3 %collective-permute-start.1 = (bf16[1,1,64,1024]{3,2,0,1:T(8,128)(2,1)S(1)}, bf16[1,1,64,1024]{3,2,0,1:T(8,128)(2,1)S(1)}, u32[]{:S(2)}, u32[]{:S(2)}) collective-permute-start(bf16[1,1,64,1024]{3,2,0,1:T(8,128)(2,1)S(1)} %get-tuple-element.251), channel_id=1, source_target_pairs={{0,8},{4,12},{8,0},{12,4},{1,9},{5,13},{9,1},{13,5},{2,10},{6,14},... | collective-permute-start | bytes 393224 | tf_op jit(solution)/shard_map/ppermute | solution.py:30
  192.8 17.4 %collective-permute-start.2 = (bf16[1,1,64,1024]{3,2,0,1:T(8,128)(2,1)S(1)}, bf16[1,1,64,1024]{3,2,0,1:T(8,128)(2,1)S(1)}, u32[]{:S(2)}, u32[]{:S(2)}) collective-permute-start(bf16[1,1,64,1024]{3,2,0,1:T(8,128)(2,1)S(1)} %get-tuple-element.250), channel_id=1, source_target_pairs={{0,12},{4,0},{8,4},{12,8},{1,13},{5,1},{9,5},{13,9},{2,14},{6,2},{... | collective-permute-start | bytes 393224 | tf_op jit(solution)/shard_map/ppermute | solution.py:30
Sparse Core Ops, SparseCore 0:
  54.9 61.5 all-gather.6
  118.0 58.9 all-gather.4
